TPU v7x, 512 devices: a whole 4x4x16 slice. The times are simulated.
512 devices in a mesh: tm: 8 (over x, core), dp: 64 (over z, y).
Axes of the slice: x: 4, y: 4, z: 16, core: 2. Of those that a mesh axis runs over, the one named last changes fastest.
Arguments:
- edge_feat: bfloat16 [8, 8192, 186], P('tm', 'dp'), may hold values from -6 to 6
- endpoint_slots: int32 [8, 2, 8192], P('tm', None, 'dp'), may hold values from 0 to 2047, as said below
- neighbor_slots: int32 [8, 20, 8192], P('tm', None, 'dp'), may hold values from 0 to 2047, as said below
- neighbor_gap: int32 [8, 20, 8192], P('tm', None, 'dp'), may hold values from 0 to 999
- score_grad: float32 [8, 8192], P('tm', 'dp'), may hold values from -1.5 to 1.5
- node_list: int32 [8, 64, 2048], P('tm', 'dp'), may hold values from 0 to 128, as said below
- memory0: float32 [8192, 256], P('dp'), may hold values from -6 to 6
- msg_weight: bfloat16 [186, 256], replicated, may hold values from -0.4375 to 0.4375
- gate_weight: bfloat16 [256, 512], replicated, may hold values from -0.375 to 0.375
- gate_bias: float32 [512], replicated, may hold values from -4 to 4
- omega: float32 [256], replicated, may hold values from 0.001 to 1
- attn_weights: bfloat16 [4, 256, 256], replicated, may hold values from -0.375 to 0.375
- pred_weights: bfloat16 [2, 256, 256], replicated, may hold values from -0.375 to 0.375
- pred_out: float32 [256], replicated, may hold values from -0.375 to 0.375
Outputs:
- scores: float32 [8, 8192], P('tm', 'dp')
- new_memory: float32 [8, 8192, 256], P('tm', 'dp')
- grad_out_proj: float32 [256, 256], replicated
- grad_pred: float32 [2, 256, 256], replicated
Inputs may be any that keep to these rules, and one draw needn't show every extreme that they name: `node_list`: each block of 32 slots (one device's requests to one owner) holds distinct rows first and 128 in the empty slots after them; every block holds at least one row; in each mini-batch some owner's block is full from every device. `endpoint_slots`: every slot points at a non-empty entry of its device's node list. `neighbor_slots`: every slot points at a non-empty entry of its device's node list.
All inputs are finite; a program needn't handle non-finite values.
Results may differ from a plain program's by a relative error of at most 0.017.
Values may be sent and summed in bfloat16 or wider, within the bound.
No kernel may reach another device: no remote copies, remote signals or barrier semaphores. Data moves between devices by JAX's collectives and lax.ppermute only.
A program may use at most 64 MiB of HBM per device.

v0:
```python
import math
import jax
import jax.numpy as jnp
from jax import lax
from jax.sharding import PartitionSpec as P

HEADS = 2


def shifted(value, axis, steps):
    count = lax.axis_size(axis)
    initial, last = (max(0, -steps), min(count, count - steps))
    return lax.ppermute(value, axis, [(source, source + steps) for source in range(initial, last)])


def local_step(
    slot_rows,
    end_slots,
    near_slots,
    near_gaps,
    cot_rows,
    omega,
    attn_weights,
    pred_weights,
    pred_out,
):
    feat_width = slot_rows.shape[1]
    events = end_slots.shape[1]
    near_count = near_slots.shape[0] // 2
    head_dim = feat_width // HEADS
    self_rows = jnp.take(slot_rows, end_slots, axis=0)
    near_rows = jnp.take(slot_rows, near_slots, axis=0).reshape(2, near_count, events, feat_width)
    phases = near_gaps.reshape(2, near_count, events).astype(jnp.float32)[..., None] * omega
    near_feat = (near_rows.astype(jnp.float32) + jnp.cos(phases)).astype(jnp.bfloat16)
    query_proj = jnp.einsum(
        "pea,ab->peb", self_rows, attn_weights[0], preferred_element_type=jnp.float32
    )
    key_proj = jnp.einsum(
        "pkea,ab->pkeb", near_feat, attn_weights[1], preferred_element_type=jnp.float32
    )
    value_proj = jnp.einsum(
        "pkea,ab->pkeb", near_feat, attn_weights[2], preferred_element_type=jnp.float32
    )
    query_heads = query_proj.reshape(2, 1, events, HEADS, head_dim)
    key_heads = key_proj.reshape(2, near_count, events, HEADS, head_dim)
    value_heads = value_proj.reshape(2, near_count, events, HEADS, head_dim)
    att_logits = jnp.sum(query_heads * key_heads, axis=-1) / math.sqrt(head_dim)
    weights_att = jax.nn.softmax(att_logits, axis=1)
    mixed_heads = (
        jnp.sum(weights_att[..., None] * value_heads, axis=1)
        .reshape(2, events, feat_width)
        .astype(jnp.bfloat16)
    )
    state_full = self_rows.astype(jnp.float32) + jnp.einsum(
        "pea,ab->peb", mixed_heads, attn_weights[3], preferred_element_type=jnp.float32
    )
    state_bf = state_full.astype(jnp.bfloat16)
    pre_pred = jnp.dot(state_bf[0], pred_weights[0], preferred_element_type=jnp.float32) + jnp.dot(
        state_bf[1], pred_weights[1], preferred_element_type=jnp.float32
    )
    sigmoid_pre = jax.nn.sigmoid(pre_pred)
    logit_out = jnp.sum(pre_pred * sigmoid_pre * pred_out, axis=-1)
    grad_pre = (
        cot_rows[:, None] * pred_out * (sigmoid_pre * (1.0 + pre_pred * (1.0 - sigmoid_pre)))
    ).astype(jnp.bfloat16)
    grad_first = jnp.einsum("ea,eb->ab", state_bf[0], grad_pre, preferred_element_type=jnp.float32)
    grad_second = jnp.einsum("ea,eb->ab", state_bf[1], grad_pre, preferred_element_type=jnp.float32)
    grad_state = jnp.einsum(
        "eb,pab->pea", grad_pre, pred_weights, preferred_element_type=jnp.float32
    ).astype(jnp.bfloat16)
    grad_out_proj = jnp.einsum(
        "pea,peb->ab", mixed_heads, grad_state, preferred_element_type=jnp.float32
    )
    return (logit_out, grad_out_proj, jnp.stack([grad_first, grad_second]))


def per_device(
    edge_feat,
    endpoint_slots,
    neighbor_slots,
    neighbor_gap,
    score_grad,
    node_list,
    memory0,
    msg_weight,
    gate_weight,
    gate_bias,
    omega,
    attn_weights,
    pred_weights,
    pred_out,
):
    groups = lax.axis_size("dp")
    node_dev, feat_width = memory0.shape
    list_len = node_list.shape[2]
    per_owner = list_len // groups
    requests = node_list[0, 0].reshape(groups, per_owner)
    wanted = lax.all_to_all(requests, "dp", split_axis=0, concat_axis=0, tiled=True)
    message = jnp.dot(edge_feat[0], msg_weight, preferred_element_type=jnp.float32).astype(
        jnp.bfloat16
    )
    message_wide = message.astype(jnp.float32)
    end_slots = endpoint_slots[0]
    flat_ends = end_slots.reshape(-1)
    slot_sums = (
        jnp.zeros((list_len, feat_width), jnp.float32)
        .at[flat_ends]
        .add(jnp.concatenate([message_wide, message_wide]))
    )
    slot_tally = jnp.zeros((list_len,), jnp.float32).at[flat_ends].add(1.0)
    got_sums, got_tally = (
        lax.all_to_all(
            slot_sums.reshape(groups, per_owner, feat_width),
            "dp",
            split_axis=0,
            concat_axis=0,
            tiled=True,
        ),
        lax.all_to_all(
            slot_tally.reshape(groups, per_owner), "dp", split_axis=0, concat_axis=0, tiled=True
        ),
    )
    picker = (wanted.reshape(-1)[:, None] == jnp.arange(node_dev)[None, :]).astype(jnp.bfloat16)
    flat_sums = got_sums.reshape(-1, feat_width)
    sums_high = flat_sums.astype(jnp.bfloat16)
    sums_low = (flat_sums - sums_high.astype(jnp.float32)).astype(jnp.bfloat16)
    totals = jnp.einsum(
        "sn,sd->nd", picker, sums_high, preferred_element_type=jnp.float32
    ) + jnp.einsum("sn,sd->nd", picker, sums_low, preferred_element_type=jnp.float32)
    counts = jnp.dot(
        got_tally.reshape(-1), picker.astype(jnp.float32), precision=lax.Precision.HIGHEST
    )
    touched = (counts > 0.5).astype(jnp.float32)
    mean_msg = (totals / jnp.maximum(counts, 1.0)[:, None]).astype(jnp.bfloat16)
    pre_gate = jnp.dot(mean_msg, gate_weight, preferred_element_type=jnp.float32) + gate_bias
    update = jax.nn.sigmoid(pre_gate[:, :feat_width]) * touched[:, None]
    candidate = jnp.tanh(pre_gate[:, feat_width:])
    decay_rate = 1.0 - update
    inject = update * candidate
    section_index = lax.axis_index("tm")
    before = memory0
    for relay_step in range(lax.axis_size("tm") - 1):
        moved_state = shifted((decay_rate * before + inject).astype(jnp.bfloat16), "tm", 1).astype(
            jnp.float32
        )
        before = jnp.where(section_index == 0, memory0, moved_state)
    new_memory = decay_rate * before + inject
    memory_bf = before.astype(jnp.bfloat16)
    full_table = lax.all_gather(memory_bf, "dp", axis=0, tiled=True)
    owner_of = jnp.arange(list_len, dtype=jnp.int32) // per_owner
    global_row = owner_of * node_dev + jnp.minimum(node_list[0, 0], node_dev - 1)
    slot_rows = jnp.take(full_table, global_row, axis=0)
    logit_out, grad_out, grad_pair = local_step(
        slot_rows,
        end_slots,
        neighbor_slots[0],
        neighbor_gap[0],
        score_grad[0],
        omega,
        attn_weights,
        pred_weights,
        pred_out,
    )
    grad_out, grad_pair = lax.psum((grad_out, grad_pair), ("tm", "dp"))
    return (logit_out[None, :], new_memory[None], grad_out, grad_pair)


def solution(mesh):
    in_specs = (
        P("tm", "dp", None),
        P("tm", None, "dp"),
        P("tm", None, "dp"),
        P("tm", None, "dp"),
        P("tm", "dp"),
        P("tm", "dp", None),
        P("dp", None),
        P(),
        P(),
        P(),
        P(),
        P(),
        P(),
        P(),
    )
    out_specs = (P("tm", "dp"), P("tm", "dp", None), P(), P())
    return jax.shard_map(
        per_device, mesh=mesh, in_specs=in_specs, out_specs=out_specs, check_vma=False
    )
```

profile of v0, /device:TPU:2, one launch (start us, length us, event | category | flops | bytes accessed | tf_op | source)
XLA Modules:
  0.0 856.8 jit_solution(11601709572848172272)
XLA Ops:
  7.7 1.4 broadcast_minimum_fusion
  9.8 18.7 %all-to-all-start = ((s32[64,1,32]{2,1,0:T(1,128)}), s32[64,1,32]{2,1,0:T(1,128)S(1)}, u32[]{:S(2)}, u32[]{:S(2)}) async-start(s32[64,1,32]{2,1,0:T(1,128)} %bitcast.2), calls=%async_computation | async-start | bytes 65536 | tf_op jit(solution)/shard_map/all_to_all | solution.py:98
  29.2 2.0 scatter_custom_fusion.1
  31.8 11.2 %all-to-all-done = s32[64,1,32]{2,1,0:T(1,128)S(1)} async-done(((s32[64,1,32]{2,1,0:T(1,128)}), s32[64,1,32]{2,1,0:T(1,128)S(1)}, u32[]{:S(2)}, u32[]{:S(2)}) %all-to-all-start) | async-done | bytes 8224 | tf_op jit(solution)/shard_map/all_to_all | solution.py:98
  43.0 4.6 all-to-all-start.2
  48.7 3.4 scatter_custom_fusion
  52.1 10.2 %all-to-all-done.2 = f32[64,1,32]{2,1,0:T(1,128)S(1)} async-done(((f32[64,1,32]{2,1,0:T(1,128)}), f32[64,1,32]{2,1,0:T(1,128)S(1)}, u32[]{:S(2)}, u32[]{:S(2)}) %all-to-all-start.2) | async-done | bytes 8224 | tf_op jit(solution)/shard_map/all_to_all | solution.py:119
  62.3 4.9 all-to-all-start.1
  70.0 95.7 %all-to-all-done.1 = f32[64,32,256]{2,1,0:T(8,128)S(1)} async-done(((f32[64,32,256]{2,1,0:T(8,128)}), f32[64,32,256]{2,1,0:T(8,128)S(1)}, u32[]{:S(2)}, u32[]{:S(2)}) %all-to-all-start.1) | async-done | bytes 2097184 | tf_op jit(solution)/shard_map/all_to_all | solution.py:112
  168.0 2.1 collective-permute-start
  170.0 3.6 collective-permute-done
  173.8 1.9 collective-permute-start.1
  175.7 3.7 collective-permute-done.1
  179.5 2.1 collective-permute-start.2
  181.5 3.7 collective-permute-done.2
  185.3 1.9 collective-permute-start.3
  187.2 3.7 collective-permute-done.3
  191.0 1.9 collective-permute-start.4
  192.9 3.7 collective-permute-done.4
  196.7 1.9 collective-permute-start.5
  198.6 3.7 collective-permute-done.5
  202.3 1.9 collective-permute-start.6
  204.3 3.7 collective-permute-done.6
  210.7 136.2 %all-gather.2.cloned.1.call-done = bf16[8192,256]{1,0:T(8,128)(2,1)} async-done(((bf16[128,256]{1,0:T(8,128)(2,1)}), bf16[8192,256]{1,0:T(8,128)(2,1)}) %all-gather.2.cloned.1.call-update) | async-done | bytes 4194320 | tf_op jit(solution)/shard_map/all_gather | solution.py:149
  346.9 9.4 %gather_fusion = bf16[2048,256]{1,0:T(8,128)(2,1)S(1)} fusion(bf16[8192,256]{1,0:T(8,128)(2,1)} %all-gather.2.cloned.1.call-done, s32[2048]{0:T(1024)S(1)} %broadcast_clamp_fusion), kind=kCustom, calls=%fused_computation | custom fusion | bytes 2105344 | tf_op jit(solution)/shard_map/jit(_take)/gather | solution.py:152
  356.7 7.6 gather_fusion.2
  364.3 1.2 gather_fusion.1
  365.8 10.1 %add_convert_fusion = bf16[20,128,256]{2,1,0:T(8,128)(2,1)S(1)} fusion(f32[256]{0:T(256)S(1)} %copy-done.10, f32[20,128]{1,0:T(8,128)S(1)} %bitcast.137, bf16[20,128,256]{2,1,0:T(8,128)(2,1)S(1)} %bitcast.127, pred[20,128]{1,0:T(8,128)(4,1)S(1)} %compare_and_fusion), kind=kLoop, calls=%fused_computation.7 | loop fusion | flops 3276800 | bytes 2635264 | tf_op jit(solution)/shard_map/convert_element_type | solution.py:34
  378.1 1.1 fusion.1
  383.4 463.0 %all-reduce.3.cloned.1.call-done = (f32[256,256]{1,0:T(8,128)}, f32[2,256,256]{2,1,0:T(8,128)}) async-done(((f32[256,256]{1,0:T(8,128)}, f32[2,256,256]{2,1,0:T(8,128)}), (f32[256,256]{1,0:T(8,128)}, f32[2,256,256]{2,1,0:T(8,128)})) %all-reduce.3.cloned.1.call-update) | async-done | bytes 786448 | tf_op jit(solution)/shard_map/psum | solution.py:164
  846.4 1.7 copy.58
  848.1 1.9 copy.59
  (86 shorter events, 18.8 us)
Async XLA Ops:
  7.2 159.7 %copy-start = (bf16[256,512]{1,0:T(8,128)(2,1)S(1)}, bf16[256,512]{1,0:T(8,128)(2,1)}, u32[]{:S(2)}) copy-start(bf16[256,512]{1,0:T(8,128)(2,1)} %param.22) | copy-start | bytes 786436
  9.8 33.3 %all-to-all-start = ((s32[64,1,32]{2,1,0:T(1,128)}), s32[64,1,32]{2,1,0:T(1,128)S(1)}, u32[]{:S(2)}, u32[]{:S(2)}) async-start(s32[64,1,32]{2,1,0:T(1,128)} %bitcast.2), calls=%async_computation | async-start | bytes 65536 | tf_op jit(solution)/shard_map/all_to_all | solution.py:98
  43.0 19.3 %all-to-all-start.2 = ((f32[64,1,32]{2,1,0:T(1,128)}), f32[64,1,32]{2,1,0:T(1,128)S(1)}, u32[]{:S(2)}, u32[]{:S(2)}) async-start(f32[64,1,32]{2,1,0:T(1,128)} %bitcast.8), calls=%async_computation.2 | async-start | bytes 65536 | tf_op jit(solution)/shard_map/all_to_all | solution.py:119
  62.3 103.4 %all-to-all-start.1 = ((f32[64,32,256]{2,1,0:T(8,128)}), f32[64,32,256]{2,1,0:T(8,128)S(1)}, u32[]{:S(2)}, u32[]{:S(2)}) async-start(f32[64,32,256]{2,1,0:T(8,128)} %bitcast.6), calls=%async_computation.1 | async-start | bytes 4194304 | tf_op jit(solution)/shard_map/all_to_all | solution.py:112
  67.2 279.7 %all-gather.2.cloned.1.call-start = ((), (), s32[]{:S(2)}) async-start(), calls=%async_computation.3 | async-start | bytes 4259840 | tf_op jit(solution)/shard_map/all_gather | solution.py:149
  70.0 96.8 %copy-start.11 = (f32[512]{0:T(512)S(1)}, f32[512]{0:T(512)}, u32[]{:S(2)}) copy-start(f32[512]{0:T(512)} %param.23) | copy-start | bytes 6148
  166.0 1.8 copy-start.1
  167.8 41.0 %copy-start.8 = (s32[1,20,128]{2,0,1:T(1,128)S(1)}, s32[1,20,128]{2,0,1:T(1,128)}, u32[]{:S(2)}) copy-start(s32[1,20,128]{2,0,1:T(1,128)} %param.17) | copy-start | bytes 30724
  167.8 41.0 %copy-start.2 = (bf16[4,256,256]{2,1,0:T(8,128)(2,1)S(1)}, bf16[4,256,256]{2,1,0:T(8,128)(2,1)}, u32[]{:S(2)}) copy-start(bf16[4,256,256]{2,1,0:T(8,128)(2,1)} %param.25) | copy-start | bytes 1572868
  168.0 5.7 collective-permute-start
  173.8 5.6 collective-permute-start.1
  179.4 31.1 %copy-start.9 = (s32[1,2,128]{2,1,0:T(2,128)S(1)}, s32[1,2,128]{2,1,0:T(2,128)}, u32[]{:S(2)}) copy-start(s32[1,2,128]{2,1,0:T(2,128)} %param.15) | copy-start | bytes 3076
  179.5 31.1 %copy-start.6 = (s32[1,20,128]{2,0,1:T(1,128)S(1)}, s32[1,20,128]{2,0,1:T(1,128)}, u32[]{:S(2)}) copy-start(s32[1,20,128]{2,0,1:T(1,128)} %param.16) | copy-start | bytes 30724
  179.5 31.2 %copy-start.7 = (s32[1,1,2048]{2,1,0:T(1,128)S(1)}, s32[1,1,2048]{2,1,0:T(1,128)}, u32[]{:S(2)}) copy-start(s32[1,1,2048]{2,1,0:T(1,128)} %param.19) | copy-start | bytes 24580
  179.5 5.7 collective-permute-start.2
  185.3 5.6 collective-permute-start.3
  191.0 5.6 collective-permute-start.4
  196.7 5.6 collective-permute-start.5
  202.3 5.6 collective-permute-start.6
  208.6 637.8 %all-reduce.3.cloned.1.call-start = ((), (), s32[]{:S(2)}) async-start(), calls=%async_computation.4 | async-start | bytes 1572864 | tf_op jit(solution)/shard_map/psum | solution.py:164
  356.7 9.0 %copy-start.10 = (f32[256]{0:T(256)S(1)}, f32[256]{0:T(256)}, u32[]{:S(2)}) copy-start(f32[256]{0:T(256)} %param.24) | copy-start | bytes 3076
  365.5 10.5 %copy-start.4 = (bf16[256,256]{1,0:T(8,128)(2,1)S(1)}, bf16[256,256]{1,0:T(8,128)(2,1)}, u32[]{:S(2)}) copy-start(bf16[256,256]{1,0:T(8,128)(2,1)} %copy.39) | copy-start | bytes 393220
  375.9 0.9 copy-start.3
  376.5 2.7 copy-start.5
  376.8 2.6 copy-start.12
  376.8 3.4 copy-start.13
Sparse Core Ops, SparseCore 0:
  208.7 138.1 all-gather.1
  382.8 463.6 all-reduce.2
where the time goes:
time: 858 us; the launch traced here: 857 us
  waiting for transfers between devices  742 us (86%)
  starting transfers between devices  42.2 us (5%)
  local copies, waits for them, and re-layouts  26.3 us (3%)
  other arithmetic  22.7 us (3%)
  between operations  14.6 us (2%)
  matrix products  9.08 us (1%)
    psum x1, waiting for transfers between devices, per_device(): grad_out, grad_pair = lax.psum((grad_out, grad_pair), ('tm', 'dp'))  463 us
    all_gather x1, waiting for transfers between devices, per_device(): full_table = lax.all_gather(memory_bf, 'dp', axis=0, tiled=True)  136 us
    all_to_all x1, waiting for transfers between devices, per_device(): lax.all_to_all(slot_sums.reshape(groups, per_owner, feat_width), 'dp', sp...  95.7 us
    ppermute x7, waiting for transfers between devices, shifted(): lax.ppermute(value, axis, [(source, source + steps) for source in range(i...  25.6 us
    all_to_all x1, starting transfers between devices, per_device(): lax.all_to_all(requests, 'dp', split_axis=0, concat_axis=0, tiled=True)  18.7 us
  transfers between devices with their start and end apart: 12, of which 12 were waited for; matrix products, arithmetic and copies ran while one was open for 1% of the time, Pallas kernels for 0%

commit v1 on v0

--- a/solution.py
+++ b/solution.py
@@ -161,7 +161,7 @@
         pred_weights,
         pred_out,
     )
-    grad_out, grad_pair = lax.psum((grad_out, grad_pair), ("tm", "dp"))
+    grad_out, grad_pair = lax.psum(lax.psum((grad_out, grad_pair), "tm"), "dp")
     return (logit_out[None, :], new_memory[None], grad_out, grad_pair)
 
 

time: 858 us -> 737 us (0.86)
  waiting for transfers between devices: 742 us -> 622 us
    psum x1 -> x2, waiting for transfers between devices: 463 us -> 343 us  [per_device(): grad_out, grad_pair = lax.psum(lax.psum((grad_out, grad_pair), 'tm'), 'dp')]
  transfers between devices with their start and end apart: 12 -> 13, of which waited for: 12 -> 13; matrix products, arithmetic and copies ran while one was open for 1% -> 2% of each run, Pallas kernels for 0% -> 0%
where the time goes in v1:
time: 737 us
  waiting for transfers between devices  622 us (84%)
  starting transfers between devices  42.2 us (6%)
  local copies, waits for them, and re-layouts  26.3 us (4%)
  other arithmetic  22.7 us (3%)
  between operations  14.3 us (2%)
  matrix products  9.08 us (1%)
    psum x2, waiting for transfers between devices, per_device(): grad_out, grad_pair = lax.psum(lax.psum((grad_out, grad_pair), 'tm'), 'dp')  343 us
    all_gather x1, waiting for transfers between devices, per_device(): full_table = lax.all_gather(memory_bf, 'dp', axis=0, tiled=True)  136 us
    all_to_all x1, waiting for transfers between devices, per_device(): lax.all_to_all(slot_sums.reshape(groups, per_owner, feat_width), 'dp', sp...  95.7 us
    ppermute x7, waiting for transfers between devices, shifted(): lax.ppermute(value, axis, [(source, source + steps) for source in range(i...  25.6 us
    all_to_all x1, starting transfers between devices, per_device(): lax.all_to_all(requests, 'dp', split_axis=0, concat_axis=0, tiled=True)  18.7 us
  transfers between devices with their start and end apart: 13, of which 13 were waited for; matrix products, arithmetic and copies ran while one was open for 2% of the time, Pallas kernels for 0%

profile of v1, /device:TPU:2, one launch (start us, length us, event | category | flops | bytes accessed | tf_op | source)
XLA Modules:
  0.0 736.7 jit_solution(6490070343468883195)
XLA Ops:
  7.7 1.4 broadcast_minimum_fusion
  9.8 18.7 %all-to-all-start = ((s32[64,1,32]{2,1,0:T(1,128)}), s32[64,1,32]{2,1,0:T(1,128)S(1)}, u32[]{:S(2)}, u32[]{:S(2)}) async-start(s32[64,1,32]{2,1,0:T(1,128)} %bitcast.2), calls=%async_computation | async-start | bytes 65536 | tf_op jit(solution)/shard_map/all_to_all | solution.py:98
  29.2 2.0 scatter_custom_fusion.1
  31.8 11.2 %all-to-all-done = s32[64,1,32]{2,1,0:T(1,128)S(1)} async-done(((s32[64,1,32]{2,1,0:T(1,128)}), s32[64,1,32]{2,1,0:T(1,128)S(1)}, u32[]{:S(2)}, u32[]{:S(2)}) %all-to-all-start) | async-done | bytes 8224 | tf_op jit(solution)/shard_map/all_to_all | solution.py:98
  43.0 4.6 all-to-all-start.2
  48.7 3.4 scatter_custom_fusion
  52.1 10.2 %all-to-all-done.2 = f32[64,1,32]{2,1,0:T(1,128)S(1)} async-done(((f32[64,1,32]{2,1,0:T(1,128)}), f32[64,1,32]{2,1,0:T(1,128)S(1)}, u32[]{:S(2)}, u32[]{:S(2)}) %all-to-all-start.2) | async-done | bytes 8224 | tf_op jit(solution)/shard_map/all_to_all | solution.py:119
  62.3 4.9 all-to-all-start.1
  70.0 95.7 %all-to-all-done.1 = f32[64,32,256]{2,1,0:T(8,128)S(1)} async-done(((f32[64,32,256]{2,1,0:T(8,128)}), f32[64,32,256]{2,1,0:T(8,128)S(1)}, u32[]{:S(2)}, u32[]{:S(2)}) %all-to-all-start.1) | async-done | bytes 2097184 | tf_op jit(solution)/shard_map/all_to_all | solution.py:112
  168.0 2.1 collective-permute-start
  170.0 3.6 collective-permute-done
  173.8 1.9 collective-permute-start.1
  175.7 3.7 collective-permute-done.1
  179.5 2.1 collective-permute-start.2
  181.6 3.7 collective-permute-done.2
  185.3 1.9 collective-permute-start.3
  187.2 3.7 collective-permute-done.3
  191.0 1.9 collective-permute-start.4
  192.9 3.7 collective-permute-done.4
  196.7 1.9 collective-permute-start.5
  198.6 3.7 collective-permute-done.5
  202.3 1.9 collective-permute-start.6
  204.3 3.7 collective-permute-done.6
  210.7 136.2 %all-gather.2.cloned.1.call-done = bf16[8192,256]{1,0:T(8,128)(2,1)} async-done(((bf16[128,256]{1,0:T(8,128)(2,1)}), bf16[8192,256]{1,0:T(8,128)(2,1)}) %all-gather.2.cloned.1.call-update) | async-done | bytes 4194320 | tf_op jit(solution)/shard_map/all_gather | solution.py:149
  346.9 9.4 %gather_fusion = bf16[2048,256]{1,0:T(8,128)(2,1)S(1)} fusion(bf16[8192,256]{1,0:T(8,128)(2,1)} %all-gather.2.cloned.1.call-done, s32[2048]{0:T(1024)S(1)} %broadcast_clamp_fusion), kind=kCustom, calls=%fused_computation | custom fusion | bytes 2105344 | tf_op jit(solution)/shard_map/jit(_take)/gather | solution.py:152
  356.8 7.6 %gather_fusion.2 = bf16[2560,256]{1,0:T(8,128)(2,1)S(1)} fusion(bf16[2048,256]{1,0:T(8,128)(2,1)S(1)} %broadcast_select_fusion, s32[3072]{0:T(1024)S(1)} %pad_clamp_fusion), kind=kCustom, calls=%fused_computation.2 | custom fusion | bytes 2631680 | tf_op jit(solution)/shard_map/jit(_take)/gather | solution.py:32
  364.3 1.2 gather_fusion.1
  365.8 10.1 %add_convert_fusion = bf16[20,128,256]{2,1,0:T(8,128)(2,1)S(1)} fusion(f32[256]{0:T(256)S(1)} %copy-done.10, f32[20,128]{1,0:T(8,128)S(1)} %bitcast.137, bf16[20,128,256]{2,1,0:T(8,128)(2,1)S(1)} %bitcast.127, pred[20,128]{1,0:T(8,128)(4,1)S(1)} %compare_and_fusion), kind=kLoop, calls=%fused_computation.7 | loop fusion | flops 3276800 | bytes 2635264 | tf_op jit(solution)/shard_map/convert_element_type | solution.py:34
  382.7 69.5 %all-reduce.7.cloned.1.call-done = (f32[256,256]{1,0:T(8,128)}, f32[2,256,256]{2,1,0:T(8,128)}) async-done(((f32[256,256]{1,0:T(8,128)}, f32[2,256,256]{2,1,0:T(8,128)}), (f32[256,256]{1,0:T(8,128)}, f32[2,256,256]{2,1,0:T(8,128)})) %all-reduce.7.cloned.1.call-update) | async-done | bytes 786448 | tf_op jit(solution)/shard_map/psum | solution.py:164
  453.0 273.7 %all-reduce.5.cloned.1.call-done = (f32[256,256]{1,0:T(8,128)}, f32[2,256,256]{2,1,0:T(8,128)}) async-done(((f32[256,256]{1,0:T(8,128)}, f32[2,256,256]{2,1,0:T(8,128)}), (f32[256,256]{1,0:T(8,128)}, f32[2,256,256]{2,1,0:T(8,128)})) %all-reduce.5.cloned.1.call-update) | async-done | bytes 786448 | tf_op jit(solution)/shard_map/psum | solution.py:164
  726.6 1.7 copy.60
  728.3 1.9 copy.61
  (89 shorter events, 20.0 us)
Async XLA Ops:
  7.2 159.7 %copy-start = (bf16[256,512]{1,0:T(8,128)(2,1)S(1)}, bf16[256,512]{1,0:T(8,128)(2,1)}, u32[]{:S(2)}) copy-start(bf16[256,512]{1,0:T(8,128)(2,1)} %param.22) | copy-start | bytes 786436
  9.8 33.3 %all-to-all-start = ((s32[64,1,32]{2,1,0:T(1,128)}), s32[64,1,32]{2,1,0:T(1,128)S(1)}, u32[]{:S(2)}, u32[]{:S(2)}) async-start(s32[64,1,32]{2,1,0:T(1,128)} %bitcast.2), calls=%async_computation | async-start | bytes 65536 | tf_op jit(solution)/shard_map/all_to_all | solution.py:98
  43.0 19.3 %all-to-all-start.2 = ((f32[64,1,32]{2,1,0:T(1,128)}), f32[64,1,32]{2,1,0:T(1,128)S(1)}, u32[]{:S(2)}, u32[]{:S(2)}) async-start(f32[64,1,32]{2,1,0:T(1,128)} %bitcast.8), calls=%async_computation.2 | async-start | bytes 65536 | tf_op jit(solution)/shard_map/all_to_all | solution.py:119
  62.3 103.4 %all-to-all-start.1 = ((f32[64,32,256]{2,1,0:T(8,128)}), f32[64,32,256]{2,1,0:T(8,128)S(1)}, u32[]{:S(2)}, u32[]{:S(2)}) async-start(f32[64,32,256]{2,1,0:T(8,128)} %bitcast.6), calls=%async_computation.1 | async-start | bytes 4194304 | tf_op jit(solution)/shard_map/all_to_all | solution.py:112
  67.2 279.7 %all-gather.2.cloned.1.call-start = ((), (), s32[]{:S(2)}) async-start(), calls=%async_computation.3 | async-start | bytes 4259840 | tf_op jit(solution)/shard_map/all_gather | solution.py:149
  70.0 96.8 %copy-start.11 = (f32[512]{0:T(512)S(1)}, f32[512]{0:T(512)}, u32[]{:S(2)}) copy-start(f32[512]{0:T(512)} %param.23) | copy-start | bytes 6148
  166.0 1.8 copy-start.1
  167.8 41.0 %copy-start.8 = (s32[1,20,128]{2,0,1:T(1,128)S(1)}, s32[1,20,128]{2,0,1:T(1,128)}, u32[]{:S(2)}) copy-start(s32[1,20,128]{2,0,1:T(1,128)} %param.17) | copy-start | bytes 30724
  167.8 41.0 %copy-start.2 = (bf16[4,256,256]{2,1,0:T(8,128)(2,1)S(1)}, bf16[4,256,256]{2,1,0:T(8,128)(2,1)}, u32[]{:S(2)}) copy-start(bf16[4,256,256]{2,1,0:T(8,128)(2,1)} %param.25) | copy-start | bytes 1572868
  168.0 5.7 collective-permute-start
  173.8 5.6 collective-permute-start.1
  179.5 31.1 %copy-start.9 = (s32[1,2,128]{2,1,0:T(2,128)S(1)}, s32[1,2,128]{2,1,0:T(2,128)}, u32[]{:S(2)}) copy-start(s32[1,2,128]{2,1,0:T(2,128)} %param.15) | copy-start | bytes 3076
  179.5 31.1 %copy-start.6 = (s32[1,20,128]{2,0,1:T(1,128)S(1)}, s32[1,20,128]{2,0,1:T(1,128)}, u32[]{:S(2)}) copy-start(s32[1,20,128]{2,0,1:T(1,128)} %param.16) | copy-start | bytes 30724
  179.5 31.2 %copy-start.7 = (s32[1,1,2048]{2,1,0:T(1,128)S(1)}, s32[1,1,2048]{2,1,0:T(1,128)}, u32[]{:S(2)}) copy-start(s32[1,1,2048]{2,1,0:T(1,128)} %param.19) | copy-start | bytes 24580
  179.5 5.7 collective-permute-start.2
  185.3 5.6 collective-permute-start.3
  191.0 5.6 collective-permute-start.4
  196.7 5.6 collective-permute-start.5
  202.3 5.6 collective-permute-start.6
  208.6 243.6 %all-reduce.7.cloned.1.call-start = ((), (), s32[]{:S(2)}) async-start(), calls=%async_computation.5 | async-start | bytes 1572864 | tf_op jit(solution)/shard_map/psum | solution.py:164
  356.7 9.0 %copy-start.10 = (f32[256]{0:T(256)S(1)}, f32[256]{0:T(256)}, u32[]{:S(2)}) copy-start(f32[256]{0:T(256)} %param.24) | copy-start | bytes 3076
  365.5 10.5 %copy-start.4 = (bf16[256,256]{1,0:T(8,128)(2,1)S(1)}, bf16[256,256]{1,0:T(8,128)(2,1)}, u32[]{:S(2)}) copy-start(bf16[256,256]{1,0:T(8,128)(2,1)} %copy.39) | copy-start | bytes 393220
  375.9 0.9 copy-start.3
  376.5 2.7 copy-start.5
  376.8 2.6 copy-start.12
  376.8 3.4 copy-start.13
  382.7 344.0 %all-reduce.5.cloned.1.call-start = ((), (), s32[]{:S(2)}) async-start(), calls=%async_computation.4 | async-start | bytes 1572864 | tf_op jit(solution)/shard_map/psum | solution.py:164
Sparse Core Ops, SparseCore 0:
  208.7 138.1 all-gather.1
  382.8 69.3 all-reduce.6
  456.0 270.6 all-reduce.4
